TPU v7x, 32 devices: a whole 2x2x4 slice. The times are simulated.
32 devices in a mesh: groups: 2 (over y), ctx: 4 (over z), mp: 4 (over x, core).
Axes of the slice: x: 2, y: 2, z: 4, core: 2. Of those that a mesh axis runs over, the one named last changes fastest.
Arguments:
- block_entry_input: bfloat16 [1536, 2048], P('mp', ('groups', 'ctx')), parts along dimension 1, may hold values from -6 to 6
- first_conv_taps: bfloat16 [3, 768, 1536], P(None, 'mp'), may hold values from -0.09375 to 0.09375
- first_pointwise_weight: bfloat16 [1536, 768], P(None, 'mp'), may hold values from -0.21875 to 0.21875
- second_conv_taps: bfloat16 [3, 768, 1536], P(None, 'mp'), may hold values from -0.09375 to 0.09375
- second_pointwise_weight: bfloat16 [1536, 768], P(None, 'mp'), may hold values from -0.21875 to 0.21875
- grad_heads: bfloat16 [8, 192, 2048], P('mp', 'ctx', 'groups'), parts along dimension 2, may hold values from -6 to 6
Outputs:
- second_block_output: bfloat16 [1536, 2048], P('mp', ('groups', 'ctx')), parts along dimension 1
- entry_input_gradient: bfloat16 [1536, 2048], P('mp', ('groups', 'ctx')), parts along dimension 1
- first_taps_gradient: float32 [6, 768, 1536], P('groups', 'mp', 'ctx'), parts along dimension 0
- first_projection_gradient: float32 [3072, 768], P(('groups', 'ctx'), 'mp'), parts along dimension 0
- second_taps_gradient: float32 [6, 768, 1536], P('groups', 'mp', 'ctx'), parts along dimension 0
- second_projection_gradient: float32 [3072, 768], P(('groups', 'ctx'), 'mp'), parts along dimension 0
There are 2 independent parts, one for each index of `groups`. A program takes and returns all parts, laid end to end along the dimension named above; an argument that names none is the same for every part. Nothing has to cross between parts.
All inputs are finite; a program needn't handle non-finite values.
Results may differ from a plain program's by a relative error of at most 0.034.
Values may be sent and summed in bfloat16 or wider, within the bound.
No kernel may reach another device: no remote copies, remote signals or barrier semaphores. Data moves between devices by JAX's collectives and lax.ppermute only.
A program may use at most 192 MiB of HBM per device.

v0:
```python
import jax
import jax.numpy as jnp
from jax import lax
from jax.sharding import PartitionSpec as P

FIRST_DILATION = 1024
SECOND_DILATION = 2048


def shifted(value, axis, by):
    length = lax.axis_size(axis)
    pairs = [(i, i + by) for i in range(length) if 0 <= i + by < length]
    return lax.ppermute(value, axis, pairs)


def gelu_slope(values):
    return jax.jvp(jax.nn.gelu, (values,), (jnp.ones_like(values),))[1]


def contract_first(left, right):
    return lax.dot_general(
        left, right, (((0,), (0,)), ((), ())), preferred_element_type=jnp.float32
    )


def contract_last(left, right):
    return lax.dot_general(
        left, right, (((1,), (1,)), ((), ())), preferred_element_type=jnp.float32
    )


def hop_steps(activations, dilation):
    return dilation // activations.shape[1]


def residual_block_forward(activations, conv_weight, point_weight, dilation):
    hop_count = hop_steps(activations, dilation)
    squash_part = jax.nn.gelu(activations.astype(jnp.float32)).astype(jnp.bfloat16)
    squashed = lax.all_gather(squash_part, "mp", axis=0, tiled=True)
    earlier = shifted(squashed, "ctx", hop_count)
    later = shifted(squashed, "ctx", -hop_count)
    pre_act = jnp.dot(conv_weight[0], earlier, preferred_element_type=jnp.float32)
    pre_act = pre_act + jnp.dot(conv_weight[1], squashed, preferred_element_type=jnp.float32)
    pre_act = pre_act + jnp.dot(conv_weight[2], later, preferred_element_type=jnp.float32)
    hidden = jax.nn.gelu(pre_act).astype(jnp.bfloat16)
    mixed = lax.psum_scatter(
        jnp.dot(point_weight, hidden, preferred_element_type=jnp.float32).astype(jnp.bfloat16),
        "mp",
        scatter_dimension=0,
        tiled=True,
    ).astype(jnp.float32)
    result = (activations.astype(jnp.float32) + mixed).astype(jnp.bfloat16)
    return (result, squashed, pre_act, hidden)


def residual_block_backward(
    incoming_gradient, activations, squashed, pre_act, hidden, conv_weight, point_weight, dilation
):
    hop_count = hop_steps(activations, dilation)
    upstream_full = lax.all_gather(incoming_gradient, "mp", axis=0, tiled=True)
    grad_hidden = contract_first(point_weight, upstream_full)
    grad_pre = (grad_hidden * gelu_slope(pre_act)).astype(jnp.bfloat16)
    grad_later = shifted(grad_pre, "ctx", -hop_count)
    grad_earlier = shifted(grad_pre, "ctx", hop_count)
    moved = (grad_later, grad_pre, grad_earlier)
    grad_conv = jnp.stack(
        [
            contract_last(moved[0], squashed),
            contract_last(moved[1], squashed),
            contract_last(moved[2], squashed),
        ]
    )
    grad_point = contract_last(upstream_full, hidden)
    total = contract_first(conv_weight[0], moved[0])
    total = total + contract_first(conv_weight[1], moved[1])
    grad_squash = lax.psum_scatter(
        (total + contract_first(conv_weight[2], moved[2])).astype(jnp.bfloat16),
        "mp",
        scatter_dimension=0,
        tiled=True,
    ).astype(jnp.float32)
    previous = (
        incoming_gradient.astype(jnp.float32)
        + grad_squash * gelu_slope(activations.astype(jnp.float32))
    ).astype(jnp.bfloat16)
    return (previous, grad_conv, grad_point)


def reduce_block(grad_conv, grad_point):
    return (
        lax.psum_scatter(
            grad_conv.astype(jnp.bfloat16), "ctx", scatter_dimension=2, tiled=True
        ).astype(jnp.float32),
        lax.psum_scatter(
            grad_point.astype(jnp.bfloat16), "ctx", scatter_dimension=0, tiled=True
        ).astype(jnp.float32),
    )


def shards(
    block_entry_input,
    first_conv_taps,
    first_pointwise_weight,
    second_conv_taps,
    second_pointwise_weight,
    grad_heads,
):
    regrouped = lax.all_to_all(grad_heads, "ctx", split_axis=2, concat_axis=1, tiled=True)
    incoming_gradient = regrouped.reshape(
        regrouped.shape[0] * regrouped.shape[1], regrouped.shape[2]
    )
    between_blocks_state, first_gelu_output, first_preactivation, first_hidden_state = (
        residual_block_forward(
            block_entry_input, first_conv_taps, first_pointwise_weight, FIRST_DILATION
        )
    )
    second_block_output, second_gelu_output, second_preactivation, second_hidden_state = (
        residual_block_forward(
            between_blocks_state, second_conv_taps, second_pointwise_weight, SECOND_DILATION
        )
    )
    incoming_gradient, conv_grad_b, point_grad_b = residual_block_backward(
        incoming_gradient,
        between_blocks_state,
        second_gelu_output,
        second_preactivation,
        second_hidden_state,
        second_conv_taps,
        second_pointwise_weight,
        SECOND_DILATION,
    )
    conv_grad_b, point_grad_b = reduce_block(conv_grad_b, point_grad_b)
    entry_input_gradient, conv_grad_a, point_grad_a = residual_block_backward(
        incoming_gradient,
        block_entry_input,
        first_gelu_output,
        first_preactivation,
        first_hidden_state,
        first_conv_taps,
        first_pointwise_weight,
        FIRST_DILATION,
    )
    conv_grad_a, point_grad_a = reduce_block(conv_grad_a, point_grad_a)
    return (
        second_block_output,
        entry_input_gradient,
        conv_grad_a,
        point_grad_a,
        conv_grad_b,
        point_grad_b,
    )


def solution(mesh):
    placed = (
        P("mp", ("groups", "ctx")),
        P(None, "mp", None),
        P(None, "mp"),
        P(None, "mp", None),
        P(None, "mp"),
        P("mp", "ctx", "groups"),
    )
    return jax.shard_map(
        shards,
        mesh=mesh,
        in_specs=placed,
        out_specs=(
            P("mp", ("groups", "ctx")),
            P("mp", ("groups", "ctx")),
            P("groups", "mp", "ctx"),
            P(("groups", "ctx"), "mp"),
            P("groups", "mp", "ctx"),
            P(("groups", "ctx"), "mp"),
        ),
        check_vma=False,
    )
```

profile of v0, /device:TPU:0, one launch (start us, length us, event | category | flops | bytes accessed | tf_op | source)
XLA Modules:
  0.0 296.0 jit_solution(17952154528425579025)
XLA Ops:
  7.2 1.2 fusion.62
  8.5 10.0 %all_gather.12 = bf16[1536,256]{1,0:T(8,128)(2,1)S(1)} all-gather(bf16[384,256]{1,0:T(8,128)(2,1)S(1)} %fusion.62), channel_id=1, replica_groups=mesh['groups'=2,'ctx'=4,'mp'=4] {'mp'}, dimensions={0}, use_global_device_ids=true | all-gather | bytes 983040 | tf_op jit(solution)/shard_map/all_gather | solution.py:39
  18.5 0.7 collective-permute-start
  19.2 1.4 fusion.33
  21.7 0.4 fusion.6
  22.1 1.2 copy.33
  23.3 24.3 %reduce-scatter.25.cloned.1.call-done = bf16[384,256]{1,0:T(8,128)(2,1)} async-done(((bf16[1536,256]{1,0:T(8,128)(2,1)}), bf16[384,256]{1,0:T(8,128)(2,1)}) %reduce-scatter.25.cloned.1.call-update) | async-done | bytes 196624 | tf_op jit(solution)/shard_map/reduce_scatter | solution.py:46
  47.6 1.1 fusion.71
  48.7 8.2 %all_gather.13 = bf16[1536,256]{1,0:T(8,128)(2,1)S(1)} all-gather(bf16[384,256]{1,0:T(8,128)(2,1)S(1)} %fusion.71), channel_id=1, replica_groups=mesh['groups'=2,'ctx'=4,'mp'=4] {'mp'}, dimensions={0}, use_global_device_ids=true | all-gather | bytes 983040 | tf_op jit(solution)/shard_map/all_gather | solution.py:39
  56.9 1.5 collective-permute-start.1
  58.4 0.4 copy.27
  58.8 1.5 reshape.35
  60.3 4.6 %all-to-all-start = ((bf16[4,2,12288]{2,1,0:T(2,128)(2,1)}), bf16[4,2,12288]{2,1,0:T(2,128)(2,1)}, u32[]{:S(2)}, u32[]{:S(2)}) async-start(bf16[4,2,12288]{2,1,0:T(2,128)(2,1)} %reshape.35), calls=%async_computation | async-start | bytes 393216 | tf_op jit(solution)/shard_map/all_to_all | solution.py:108
  64.9 1.4 fusion.23
  66.3 1.6 fusion.19
  68.0 1.6 fusion.16
  69.6 0.4 fusion.7
  70.1 1.2 copy.35
  71.3 1.7 all-to-all-done
  73.0 1.4 reshape.36
  74.4 0.4 copy.32
  74.9 0.7 copy-done.8
  75.6 8.0 %all_gather.14 = bf16[1536,256]{1,0:T(8,128)(2,1)S(1)} all-gather(bf16[384,256]{1,0:T(8,128)(2,1)S(1)} %bitcast.104), channel_id=1, replica_groups=mesh['groups'=2,'ctx'=4,'mp'=4] {'mp'}, dimensions={0}, use_global_device_ids=true | all-gather | bytes 983040 | tf_op jit(solution)/shard_map/all_gather | solution.py:60
  83.9 0.7 collective-permute-start.2
  84.6 0.4 fusion.21
  85.1 0.4 fusion.17
  85.7 0.4 fusion.5
  86.1 1.2 copy.37
  87.3 1.7 fusion.12
  89.0 1.2 copy.47
  90.2 5.3 %reduce-scatter.27.cloned.1.call-done = bf16[384,256]{1,0:T(8,128)(2,1)} async-done(((bf16[1536,256]{1,0:T(8,128)(2,1)}), bf16[384,256]{1,0:T(8,128)(2,1)}) %reduce-scatter.27.cloned.1.call-update) | async-done | bytes 196624 | tf_op jit(solution)/shard_map/reduce_scatter | solution.py:46
  95.5 26.4 %reduce-scatter.29.cloned.1.call-done = bf16[384,256]{1,0:T(8,128)(2,1)} async-done(((bf16[1536,256]{1,0:T(8,128)(2,1)}), bf16[384,256]{1,0:T(8,128)(2,1)}) %reduce-scatter.29.cloned.1.call-update) | async-done | bytes 196624 | tf_op jit(solution)/shard_map/reduce_scatter | solution.py:76
  121.9 2.1 fusion.76
  124.1 8.2 %all_gather.15 = bf16[1536,256]{1,0:T(8,128)(2,1)S(1)} all-gather(bf16[384,256]{1,0:T(8,128)(2,1)S(1)} %get-tuple-element.24), channel_id=1, replica_groups=mesh['groups'=2,'ctx'=4,'mp'=4] {'mp'}, dimensions={0}, use_global_device_ids=true | all-gather | bytes 983040 | tf_op jit(solution)/shard_map/all_gather | solution.py:60
  132.3 1.2 convolution_convert_fusion.5
  133.5 2.2 copy.43
  135.8 1.5 fusion.88
  137.3 0.7 collective-permute-start.3
  138.8 0.4 fusion.4
  139.2 1.2 copy.39
  140.6 0.4 fusion.11
  141.1 0.4 fusion.10
  141.7 3.5 %copy.45 = bf16[3,192,1536]{1,0,2:T(4,128)(2,1)} copy(bf16[3,192,1536]{2,1,0:T(8,128)(2,1)S(1)} %pad_maximum_fusion.1) | data formatting | bytes 3538944
  145.3 7.0 %reshape.31 = bf16[1536,576]{1,0:T(8,128)(2,1)} reshape(bf16[1536,3,192]{2,1,0:T(4,128)(2,1)} %bitcast.98) | data formatting | bytes 3538944
  152.4 0.8 copy-done.16
  153.2 0.4 fusion.9
  153.6 0.4 fusion.8
  154.2 3.5 %copy.41 = bf16[3,192,1536]{1,0,2:T(4,128)(2,1)} copy(bf16[3,192,1536]{2,1,0:T(8,128)(2,1)S(1)} %pad_maximum_fusion) | data formatting | bytes 3538944
  157.8 7.1 %reshape.27 = bf16[1536,576]{1,0:T(8,128)(2,1)} reshape(bf16[1536,3,192]{2,1,0:T(4,128)(2,1)} %bitcast.99) | data formatting | bytes 3538944
  164.9 1.1 copy.48
  166.0 0.7 convert_element_type.137
  166.7 6.2 %reduce-scatter.35.cloned.1.call-done = bf16[384,192]{1,0:T(8,128)(2,1)} async-done(((bf16[1536,192]{1,0:T(8,128)(2,1)}), bf16[384,192]{1,0:T(8,128)(2,1)}) %reduce-scatter.35.cloned.1.call-update) | async-done | bytes 147472
  173.0 1.1 copy.44
  174.0 0.7 convert_element_type.133
  174.8 23.9 %reduce-scatter.31.cloned.1.call-done = bf16[384,256]{1,0:T(8,128)(2,1)} async-done(((bf16[1536,256]{1,0:T(8,128)(2,1)}), bf16[384,256]{1,0:T(8,128)(2,1)}) %reduce-scatter.31.cloned.1.call-update) | async-done | bytes 196624 | tf_op jit(solution)/shard_map/reduce_scatter | solution.py:76
  198.7 1.9 fusion.67
  200.6 41.9 %reduce-scatter.37.cloned.1.call-done = bf16[384,576]{1,0:T(8,128)(2,1)} async-done(((bf16[1536,576]{1,0:T(8,128)(2,1)}), bf16[384,576]{1,0:T(8,128)(2,1)}) %reduce-scatter.37.cloned.1.call-update) | async-done | bytes 442384
  242.5 1.8 reshape.32
  244.3 0.9 copy.46
  245.2 1.0 convert_element_type.134
  246.1 39.4 %reduce-scatter.33.cloned.1.call-done = bf16[384,576]{1,0:T(8,128)(2,1)} async-done(((bf16[1536,576]{1,0:T(8,128)(2,1)}), bf16[384,576]{1,0:T(8,128)(2,1)}) %reduce-scatter.33.cloned.1.call-update) | async-done | bytes 442384
  285.5 1.8 reshape.28
  287.3 0.9 copy.42
  288.2 1.0 convert_element_type.131
  (63 shorter events, 3.5 us)
Async XLA Ops:
  7.2 62.5 %copy-start = (bf16[1536,192]{0,1:T(8,128)(2,1)S(1)}, bf16[1536,192]{0,1:T(8,128)(2,1)}, u32[]{:S(2)}) copy-start(bf16[1536,192]{0,1:T(8,128)(2,1)} %param.10) | copy-start | bytes 1769476
  7.2 13.4 %copy-start.2 = (bf16[3,192,1536]{2,1,0:T(8,128)(2,1)S(1)}, bf16[3,192,1536]{2,1,0:T(8,128)(2,1)}, u32[]{:S(2)}) copy-start(bf16[3,192,1536]{2,1,0:T(8,128)(2,1)} %param.7) | copy-start | bytes 5308420
  7.2 40.4 %reduce-scatter.25.cloned.1.call-start = ((), (), s32[]{:S(2)}) async-start(), calls=%async_computation.9 | async-start | bytes 983040 | tf_op jit(solution)/shard_map/reduce_scatter | solution.py:46
  18.5 2.1 collective-permute-start
  20.6 1.1 copy-start.12
  21.7 25.9 %copy-start.5 = (bf16[384,256]{1,0:T(8,128)(2,1)S(1)}, bf16[384,256]{1,0:T(8,128)(2,1)}, u32[]{:S(2)}) copy-start(bf16[384,256]{1,0:T(8,128)(2,1)} %param.6) | copy-start | bytes 589828
  22.1 36.3 %copy-start.17 = (bf16[2,48,1024]{2,1,0:T(8,128)(2,1)S(1)}, bf16[2,48,1024]{2,1,0:T(8,128)(2,1)}, u32[]{:S(2)}) copy-start(bf16[2,48,1024]{2,1,0:T(8,128)(2,1)} %param.11) | copy-start | bytes 589828
  56.9 9.4 %collective-permute-start.1 = (bf16[1536,256]{1,0:T(8,128)(2,1)S(1)}, bf16[1536,256]{1,0:T(8,128)(2,1)}, u32[]{:S(2)}, u32[]{:S(2)}) collective-permute-start(bf16[1536,256]{1,0:T(8,128)(2,1)S(1)} %all_gather.13), channel_id=1, source_target_pairs={} | collective-permute-start | bytes 2359304 | tf_op jit(solution)/shard_map/ppermute | solution.py:13
  60.3 12.7 %all-to-all-start = ((bf16[4,2,12288]{2,1,0:T(2,128)(2,1)}), bf16[4,2,12288]{2,1,0:T(2,128)(2,1)}, u32[]{:S(2)}, u32[]{:S(2)}) async-start(bf16[4,2,12288]{2,1,0:T(2,128)(2,1)} %reshape.35), calls=%async_computation | async-start | bytes 393216 | tf_op jit(solution)/shard_map/all_to_all | solution.py:108
  64.9 30.6 %reduce-scatter.27.cloned.1.call-start = ((), (), s32[]{:S(2)}) async-start(), calls=%async_computation.10 | async-start | bytes 983040 | tf_op jit(solution)/shard_map/reduce_scatter | solution.py:46
  71.2 50.7 %reduce-scatter.29.cloned.1.call-start = ((), (), s32[]{:S(2)}) async-start(), calls=%async_computation.11 | async-start | bytes 983040 | tf_op jit(solution)/shard_map/reduce_scatter | solution.py:76
  74.9 9.7 %copy-start.1 = (bf16[3,192,1536]{2,1,0:T(8,128)(2,1)S(1)}, bf16[3,192,1536]{2,1,0:T(8,128)(2,1)}, u32[]{:S(2)}) copy-start(bf16[3,192,1536]{2,1,0:T(8,128)(2,1)} %param.9) | copy-start | bytes 5308420
  74.9 0.7 copy-start.8
  83.6 1.4 copy-start.4
  83.9 1.1 copy-start.13
  83.9 1.1 collective-permute-start.2
  85.0 0.6 copy-start.10
  87.3 34.7 %copy-start.9 = (bf16[2,4,48,256]{3,2,1,0:T(8,128)(2,1)S(1)}, bf16[2,4,48,256]{3,2,1,0:T(8,128)(2,1)}, u32[]{:S(2)}) copy-start(bf16[2,4,48,256]{3,2,1,0:T(8,128)(2,1)} %copy-done.8) | copy-start | bytes 589828
  87.3 77.6 %reduce-scatter.39.cloned.1.call-start = ((), (), s32[]{:S(2)}) async-start(), calls=%async_computation.16 | async-start | bytes 983040
  90.2 82.8 %reduce-scatter.35.cloned.1.call-start = ((), (), s32[]{:S(2)}) async-start(), calls=%async_computation.14 | async-start | bytes 983040
  124.1 11.7 %copy-start.6 = (bf16[384,256]{1,0:T(8,128)(2,1)}, bf16[384,256]{1,0:T(8,128)(2,1)S(1)}, u32[]{:S(2)}) copy-start(bf16[384,256]{1,0:T(8,128)(2,1)S(1)} %get-tuple-element.24) | copy-start | bytes 589828
  135.7 62.9 %reduce-scatter.31.cloned.1.call-start = ((), (), s32[]{:S(2)}) async-start(), calls=%async_computation.12 | async-start | bytes 983040 | tf_op jit(solution)/shard_map/reduce_scatter | solution.py:76
  135.8 2.2 copy-start.3
  137.3 1.5 copy-start.15
  137.3 1.1 collective-permute-start.3
  139.2 1.4 copy-start.14
  139.2 1.9 copy-start.11
  140.4 102.1 %reduce-scatter.37.cloned.1.call-start = ((), (), s32[]{:S(2)}) async-start(), calls=%async_computation.15 | async-start | bytes 2457600
  152.3 0.9 copy-start.16
  152.3 133.2 %reduce-scatter.33.cloned.1.call-start = ((), (), s32[]{:S(2)}) async-start(), calls=%async_computation.13 | async-start | bytes 2457600
  164.8 33.8 %copy-start.7 = (bf16[384,256]{1,0:T(8,128)(2,1)S(1)}, bf16[384,256]{1,0:T(8,128)(2,1)}, u32[]{:S(2)}) copy-start(bf16[384,256]{1,0:T(8,128)(2,1)} %copy-done.6) | copy-start | bytes 589828
Sparse Core Ops, SparseCore 0:
  23.4 24.1 reduce-scatter.24
  71.4 24.1 reduce-scatter.26
  98.6 23.2 reduce-scatter.28
  124.2 23.3 reduce-scatter.38
  150.4 22.5 reduce-scatter.34
  176.1 22.5 reduce-scatter.30
  201.0 41.4 reduce-scatter.36
  244.8 40.6 reduce-scatter.32
where the time goes:
time: 297 us; the launch traced here: 296 us
  waiting for transfers between devices  169 us (57%)
  local copies, waits for them, and re-layouts  42.7 us (14%)
  blocking collectives  34.5 us (12%)
  matrix products  16.2 us (5%)
  between operations  14.6 us (5%)
  other arithmetic  10.2 us (3%)
  starting transfers between devices  8.6 us (3%)
    unnamed x12, waiting for transfers between devices  87.6 us
    reduce_scatter x2, waiting for transfers between devices, residual_block_backward(): lax.psum_scatter((total + contract_first(conv_weight[2], moved[2])).astyp...  50.3 us
    unnamed x55, local copies, waits for them, and re-layouts  42.3 us
    reduce_scatter x2, waiting for transfers between devices, residual_block_forward(): lax.psum_scatter(jnp.dot(point_weight, hidden, preferred_element_type=jnp...  29.6 us
    all_gather x2, blocking collectives, residual_block_forward(): squashed = lax.all_gather(squash_part, 'mp', axis=0, tiled=True)  18.3 us
    all_gather x2, blocking collectives, residual_block_backward(): upstream_full = lax.all_gather(incoming_gradient, 'mp', axis=0, tiled=True)  16.2 us
  transfers between devices with their start and end apart: 13, of which 8 were waited for; matrix products, arithmetic and copies ran while one was open for 20% of the time, Pallas kernels for 0%

commit v1 on v0

--- a/solution.py
+++ b/solution.py
@@ -105,7 +105,14 @@
     second_pointwise_weight,
     grad_heads,
 ):
-    regrouped = lax.all_to_all(grad_heads, "ctx", split_axis=2, concat_axis=1, tiled=True)
+
+    def units_meet(sample):
+        z2 = jnp.concatenate(
+            lax.all_to_all(jnp.stack(jnp.split(sample, lax.psum(1, "ctx"), 2), 0), "ctx", 0, 0), 1
+        )
+        return z2
+
+    regrouped = units_meet(grad_heads)
     incoming_gradient = regrouped.reshape(
         regrouped.shape[0] * regrouped.shape[1], regrouped.shape[2]
     )

time: 297 us -> 296 us (level)
    unnamed x55 -> x50, local copies, waits for them, and re-layouts: 42.3 us -> 38.8 us
  transfers between devices with their start and end apart: 13 -> 13, of which waited for: 8 -> 8; matrix products, arithmetic and copies ran while one was open for 20% -> 19% of each run, Pallas kernels for 0% -> 0%
where the time goes in v1:
time: 296 us; the launch traced here: 294 us
  waiting for transfers between devices  170 us (57%)
  local copies, waits for them, and re-layouts  40.7 us (14%)
  blocking collectives  34.4 us (12%)
  matrix products  15.7 us (5%)
  between operations  14.6 us (5%)
  other arithmetic  10.9 us (4%)
  starting transfers between devices  7.77 us (3%)
    unnamed x12, waiting for transfers between devices  87.8 us
    reduce_scatter x2, waiting for transfers between devices, residual_block_backward(): lax.psum_scatter((total + contract_first(conv_weight[2], moved[2])).astyp...  50.3 us
    unnamed x50, local copies, waits for them, and re-layouts  38.8 us
    reduce_scatter x2, waiting for transfers between devices, residual_block_forward(): lax.psum_scatter(jnp.dot(point_weight, hidden, preferred_element_type=jnp...  30 us
    all_gather x2, blocking collectives, residual_block_forward(): squashed = lax.all_gather(squash_part, 'mp', axis=0, tiled=True)  18.3 us
    all_gather x2, blocking collectives, residual_block_backward(): upstream_full = lax.all_gather(incoming_gradient, 'mp', axis=0, tiled=True)  16.2 us
  transfers between devices with their start and end apart: 13, of which 8 were waited for; matrix products, arithmetic and copies ran while one was open for 19% of the time, Pallas kernels for 0%

profile of v1, /device:TPU:0, one launch (start us, length us, event | category | flops | bytes accessed | tf_op | source)
XLA Modules:
  0.0 294.4 jit_solution(13335595561705027763)
XLA Ops:
  7.2 1.2 fusion.61
  8.5 10.0 %all_gather.12 = bf16[1536,256]{1,0:T(8,128)(2,1)S(1)} all-gather(bf16[384,256]{1,0:T(8,128)(2,1)S(1)} %fusion.61), channel_id=1, replica_groups=mesh['groups'=2,'ctx'=4,'mp'=4] {'mp'}, dimensions={0}, use_global_device_ids=true | all-gather | bytes 983040 | tf_op jit(solution)/shard_map/all_gather | solution.py:39
  18.5 0.7 collective-permute-start
  19.2 1.4 fusion.32
  21.7 0.4 fusion.6
  22.1 1.2 copy.25
  23.3 24.3 %reduce-scatter.25.cloned.1.call-done = bf16[384,256]{1,0:T(8,128)(2,1)} async-done(((bf16[1536,256]{1,0:T(8,128)(2,1)}), bf16[384,256]{1,0:T(8,128)(2,1)}) %reduce-scatter.25.cloned.1.call-update) | async-done | bytes 196624 | tf_op jit(solution)/shard_map/reduce_scatter | solution.py:46
  47.6 1.1 fusion.70
  48.7 8.2 %all_gather.13 = bf16[1536,256]{1,0:T(8,128)(2,1)S(1)} all-gather(bf16[384,256]{1,0:T(8,128)(2,1)S(1)} %fusion.70), channel_id=1, replica_groups=mesh['groups'=2,'ctx'=4,'mp'=4] {'mp'}, dimensions={0}, use_global_device_ids=true | all-gather | bytes 983040 | tf_op jit(solution)/shard_map/all_gather | solution.py:39
  56.9 0.7 collective-permute-start.1
  57.6 0.9 slice_bitcast_fusion.3
  58.5 0.7 pad_maximum_fusion.2
  59.2 4.6 %all-to-all-start = ((bf16[4,2,48,256]{3,2,1,0:T(8,128)(2,1)}), bf16[4,2,48,256]{3,2,1,0:T(8,128)(2,1)}, u32[]{:S(2)}, u32[]{:S(2)}) async-start(bf16[4,2,48,256]{3,2,1,0:T(8,128)(2,1)} %pad_maximum_fusion.2), calls=%async_computation | async-start | bytes 393216 | tf_op jit(solution)/shard_map/all_to_all | solution.py:111
  63.8 1.4 fusion.22
  65.2 1.4 fusion.18
  66.6 1.4 fusion.15
  68.0 0.4 fusion.7
  68.4 1.2 copy.27
  69.6 2.2 all-to-all-done
  71.9 1.1 copy.22
  73.0 0.7 copy-done.8
  73.6 8.0 %all_gather.14 = bf16[1536,256]{1,0:T(8,128)(2,1)S(1)} all-gather(bf16[384,256]{1,0:T(8,128)(2,1)S(1)} %bitcast.108), channel_id=1, replica_groups=mesh['groups'=2,'ctx'=4,'mp'=4] {'mp'}, dimensions={0}, use_global_device_ids=true | all-gather | bytes 983040 | tf_op jit(solution)/shard_map/all_gather | solution.py:60
  82.0 0.7 collective-permute-start.2
  82.7 0.4 fusion.20
  83.1 0.4 fusion.16
  83.7 0.4 fusion.5
  84.1 1.2 copy.29
  85.3 1.6 convolution_convert_fusion.2
  86.9 1.2 copy.39
  88.2 5.7 %reduce-scatter.27.cloned.1.call-done = bf16[384,256]{1,0:T(8,128)(2,1)} async-done(((bf16[1536,256]{1,0:T(8,128)(2,1)}), bf16[384,256]{1,0:T(8,128)(2,1)}) %reduce-scatter.27.cloned.1.call-update) | async-done | bytes 196624 | tf_op jit(solution)/shard_map/reduce_scatter | solution.py:46
  93.9 26.4 %reduce-scatter.29.cloned.1.call-done = bf16[384,256]{1,0:T(8,128)(2,1)} async-done(((bf16[1536,256]{1,0:T(8,128)(2,1)}), bf16[384,256]{1,0:T(8,128)(2,1)}) %reduce-scatter.29.cloned.1.call-update) | async-done | bytes 196624 | tf_op jit(solution)/shard_map/reduce_scatter | solution.py:76
  120.3 2.1 fusion.75
  122.5 8.2 %all_gather.15 = bf16[1536,256]{1,0:T(8,128)(2,1)S(1)} all-gather(bf16[384,256]{1,0:T(8,128)(2,1)S(1)} %get-tuple-element.18), channel_id=1, replica_groups=mesh['groups'=2,'ctx'=4,'mp'=4] {'mp'}, dimensions={0}, use_global_device_ids=true | all-gather | bytes 983040 | tf_op jit(solution)/shard_map/all_gather | solution.py:60
  130.6 1.2 convolution_convert_fusion.5
  131.9 2.2 copy.35
  134.2 1.5 fusion.87
  135.7 0.7 collective-permute-start.3
  136.4 0.4 fusion.30
  137.2 0.4 fusion.4
  137.6 1.2 copy.31
  138.8 0.4 fusion.11
  139.3 0.4 fusion.10
  139.9 3.5 %copy.37 = bf16[3,192,1536]{1,0,2:T(4,128)(2,1)} copy(bf16[3,192,1536]{2,1,0:T(8,128)(2,1)S(1)} %pad_maximum_fusion.1) | data formatting | bytes 3538944
  143.4 7.0 %reshape.30 = bf16[1536,576]{1,0:T(8,128)(2,1)} reshape(bf16[1536,3,192]{2,1,0:T(4,128)(2,1)} %bitcast.104) | data formatting | bytes 3538944
  150.7 0.6 copy-done.16
  151.4 0.4 fusion.9
  151.8 0.4 fusion.8
  152.4 3.5 %copy.33 = bf16[3,192,1536]{1,0,2:T(4,128)(2,1)} copy(bf16[3,192,1536]{2,1,0:T(8,128)(2,1)S(1)} %pad_maximum_fusion) | data formatting | bytes 3538944
  156.0 7.1 %reshape.26 = bf16[1536,576]{1,0:T(8,128)(2,1)} reshape(bf16[1536,3,192]{2,1,0:T(4,128)(2,1)} %bitcast.105) | data formatting | bytes 3538944
  163.1 1.1 copy.40
  164.2 0.7 convert_element_type.133
  164.9 6.4 %reduce-scatter.35.cloned.1.call-done = bf16[384,192]{1,0:T(8,128)(2,1)} async-done(((bf16[1536,192]{1,0:T(8,128)(2,1)}), bf16[384,192]{1,0:T(8,128)(2,1)}) %reduce-scatter.35.cloned.1.call-update) | async-done | bytes 147472
  171.3 1.1 copy.36
  172.4 0.7 convert_element_type.130
  173.2 23.9 %reduce-scatter.31.cloned.1.call-done = bf16[384,256]{1,0:T(8,128)(2,1)} async-done(((bf16[1536,256]{1,0:T(8,128)(2,1)}), bf16[384,256]{1,0:T(8,128)(2,1)}) %reduce-scatter.31.cloned.1.call-update) | async-done | bytes 196624 | tf_op jit(solution)/shard_map/reduce_scatter | solution.py:76
  197.0 1.9 fusion.66
  198.9 41.9 %reduce-scatter.37.cloned.1.call-done = bf16[384,576]{1,0:T(8,128)(2,1)} async-done(((bf16[1536,576]{1,0:T(8,128)(2,1)}), bf16[384,576]{1,0:T(8,128)(2,1)}) %reduce-scatter.37.cloned.1.call-update) | async-done | bytes 442384
  240.8 1.8 reshape.31
  242.6 0.9 copy.38
  243.5 1.0 convert_element_type.131
  244.5 39.3 %reduce-scatter.33.cloned.1.call-done = bf16[384,576]{1,0:T(8,128)(2,1)} async-done(((bf16[1536,576]{1,0:T(8,128)(2,1)}), bf16[384,576]{1,0:T(8,128)(2,1)}) %reduce-scatter.33.cloned.1.call-update) | async-done | bytes 442384
  283.8 1.8 reshape.27
  285.7 0.9 copy.34
  286.6 1.0 convert_element_type.128
  (59 shorter events, 3.1 us)
Async XLA Ops:
  7.2 60.8 %copy-start = (bf16[1536,192]{0,1:T(8,128)(2,1)S(1)}, bf16[1536,192]{0,1:T(8,128)(2,1)}, u32[]{:S(2)}) copy-start(bf16[1536,192]{0,1:T(8,128)(2,1)} %param.10) | copy-start | bytes 1769476
  7.2 13.4 %copy-start.2 = (bf16[3,192,1536]{2,1,0:T(8,128)(2,1)S(1)}, bf16[3,192,1536]{2,1,0:T(8,128)(2,1)}, u32[]{:S(2)}) copy-start(bf16[3,192,1536]{2,1,0:T(8,128)(2,1)} %param.7) | copy-start | bytes 5308420
  7.2 40.4 %reduce-scatter.25.cloned.1.call-start = ((), (), s32[]{:S(2)}) async-start(), calls=%async_computation.9 | async-start | bytes 983040 | tf_op jit(solution)/shard_map/reduce_scatter | solution.py:46
  18.5 2.1 collective-permute-start
  20.6 1.1 copy-start.12
  21.7 25.9 %copy-start.5 = (bf16[384,256]{1,0:T(8,128)(2,1)S(1)}, bf16[384,256]{1,0:T(8,128)(2,1)}, u32[]{:S(2)}) copy-start(bf16[384,256]{1,0:T(8,128)(2,1)} %param.6) | copy-start | bytes 589828
  56.9 8.3 %collective-permute-start.1 = (bf16[1536,256]{1,0:T(8,128)(2,1)S(1)}, bf16[1536,256]{1,0:T(8,128)(2,1)S(1)}, u32[]{:S(2)}, u32[]{:S(2)}) collective-permute-start(bf16[1536,256]{1,0:T(8,128)(2,1)S(1)} %all_gather.13), channel_id=1, source_target_pairs={} | collective-permute-start | bytes 2359304 | tf_op jit(solution)/shard_map/ppermute | solution.py:13
  59.2 12.7 %all-to-all-start = ((bf16[4,2,48,256]{3,2,1,0:T(8,128)(2,1)}), bf16[4,2,48,256]{3,2,1,0:T(8,128)(2,1)}, u32[]{:S(2)}, u32[]{:S(2)}) async-start(bf16[4,2,48,256]{3,2,1,0:T(8,128)(2,1)} %pad_maximum_fusion.2), calls=%async_computation | async-start | bytes 393216 | tf_op jit(solution)/shard_map/all_to_all | solution.py:111
  63.8 30.1 %reduce-scatter.27.cloned.1.call-start = ((), (), s32[]{:S(2)}) async-start(), calls=%async_computation.10 | async-start | bytes 983040 | tf_op jit(solution)/shard_map/reduce_scatter | solution.py:46
  69.6 50.7 %reduce-scatter.29.cloned.1.call-start = ((), (), s32[]{:S(2)}) async-start(), calls=%async_computation.11 | async-start | bytes 983040 | tf_op jit(solution)/shard_map/reduce_scatter | solution.py:76
  71.9 10.8 %copy-start.1 = (bf16[3,192,1536]{2,1,0:T(8,128)(2,1)S(1)}, bf16[3,192,1536]{2,1,0:T(8,128)(2,1)}, u32[]{:S(2)}) copy-start(bf16[3,192,1536]{2,1,0:T(8,128)(2,1)} %param.9) | copy-start | bytes 5308420
  72.9 0.7 copy-start.8
  81.6 1.4 copy-start.4
  82.0 1.1 copy-start.13
  82.0 1.1 collective-permute-start.2
  83.1 0.6 copy-start.10
  85.3 35.0 %copy-start.9 = (bf16[4,2,48,256]{3,2,0,1:T(8,128)(2,1)S(1)}, bf16[4,2,48,256]{3,2,0,1:T(8,128)(2,1)}, u32[]{:S(2)}) copy-start(bf16[4,2,48,256]{3,2,0,1:T(8,128)(2,1)} %copy-done.8) | copy-start | bytes 589828
  85.3 77.8 %reduce-scatter.39.cloned.1.call-start = ((), (), s32[]{:S(2)}) async-start(), calls=%async_computation.16 | async-start | bytes 983040
  88.1 83.2 %reduce-scatter.35.cloned.1.call-start = ((), (), s32[]{:S(2)}) async-start(), calls=%async_computation.14 | async-start | bytes 983040
  122.5 11.6 %copy-start.6 = (bf16[384,256]{1,0:T(8,128)(2,1)}, bf16[384,256]{1,0:T(8,128)(2,1)S(1)}, u32[]{:S(2)}) copy-start(bf16[384,256]{1,0:T(8,128)(2,1)S(1)} %get-tuple-element.18) | copy-start | bytes 589828
  134.1 62.9 %reduce-scatter.31.cloned.1.call-start = ((), (), s32[]{:S(2)}) async-start(), calls=%async_computation.12 | async-start | bytes 983040 | tf_op jit(solution)/shard_map/reduce_scatter | solution.py:76
  134.1 2.2 copy-start.3
  135.7 1.5 copy-start.15
  135.7 1.1 collective-permute-start.3
  137.6 1.3 copy-start.14
  137.6 1.7 copy-start.11
  138.8 102.1 %reduce-scatter.37.cloned.1.call-start = ((), (), s32[]{:S(2)}) async-start(), calls=%async_computation.15 | async-start | bytes 2457600
  150.5 0.9 copy-start.16
  150.5 133.3 %reduce-scatter.33.cloned.1.call-start = ((), (), s32[]{:S(2)}) async-start(), calls=%async_computation.13 | async-start | bytes 2457600
  163.0 34.0 %copy-start.7 = (bf16[384,256]{1,0:T(8,128)(2,1)S(1)}, bf16[384,256]{1,0:T(8,128)(2,1)}, u32[]{:S(2)}) copy-start(bf16[384,256]{1,0:T(8,128)(2,1)} %copy-done.6) | copy-start | bytes 589828
Sparse Core Ops, SparseCore 0:
  23.4 24.1 reduce-scatter.24
  69.7 24.1 reduce-scatter.26
  97.0 23.2 reduce-scatter.28
  122.6 23.3 reduce-scatter.38
  148.8 22.5 reduce-scatter.34
  174.5 22.4 reduce-scatter.30
  199.3 41.4 reduce-scatter.36
  243.1 40.6 reduce-scatter.32
